TPU v7x, 512 devices: a whole 4x8x8 slice. The times are simulated.
512 devices in a mesh: row: 32 (over z, y_lo), col: 16 (over y_hi, x, core).
Axes of the slice: x: 4, y: 8 (y_hi: 2, y_lo: 4; y = y_hi * 4 + y_lo), z: 8, core: 2. Of those that a mesh axis runs over, the one named last changes fastest.
Arguments:
- features: bfloat16 [16, 4096, 128], P('col', 'row'), may hold values from -6 to 6
- weight1: bfloat16 [128, 128], replicated, may hold values from -0.5 to 0.5
- weight2: bfloat16 [128, 128], replicated, may hold values from -0.5 to 0.5
- tile_values: bfloat16 [32, 16, 96, 128, 128], P('row', 'col'), may hold values from -0.1875 to 0.1875
- tile_coords: int32 [32, 16, 2, 96], P('row', 'col'), may hold values from 0 to 31, as said below
- tile_count: int32 [32, 16], P('row', 'col'), may hold values from 1 to 96, as said below
- out_grad: bfloat16 [16, 4096, 128], P('col', 'row'), may hold values from -6 to 6
Outputs:
- output: bfloat16 [16, 4096, 128], P('col', 'row')
- grad_features: bfloat16 [16, 4096, 128], P('col', 'row')
- grad_weight1: float32 [128, 128], replicated
- grad_weight2: float32 [128, 128], replicated
Inputs may be any that keep to these rules, and one draw needn't show every extreme that they name: On each device tile_coords[r, c, 0, t] is below 16 and tile_coords[r, c, 1, t] below 32; no block position appears twice among a device's 96 slots. `tile_count`: some device has all 96 slots live.
All inputs are finite; a program needn't handle non-finite values.
Results may differ from a plain program's by a relative error of at most 0.034.
Values may be sent and summed in bfloat16 or wider, within the bound.
No kernel may reach another device: no remote copies, remote signals or barrier semaphores. Data moves between devices by JAX's collectives and lax.ppermute only.
A program may use at most 64 MiB of HBM per device.

v0:
```python
import math
import jax
import jax.numpy as jnp
from jax import lax
from jax.sharding import PartitionSpec as P


def forward_part(local_tiles, row_ids, col_ids, live_slots, panel_rows, row_blocks):
    block_side = local_tiles.shape[1]
    feat_width = panel_rows.shape[-1]
    blocks = panel_rows.reshape(-1, block_side, feat_width)[col_ids]
    products = jnp.einsum("tij,tjf->tif", local_tiles, blocks, preferred_element_type=jnp.float32)
    onehot = jnp.where(
        (row_ids[None, :] == jnp.arange(row_blocks, dtype=jnp.int32)[:, None])
        & live_slots[None, :],
        1.0,
        0.0,
    ).astype(jnp.float32)
    return jnp.einsum("rt,tif->rif", onehot, products).reshape(row_blocks * block_side, feat_width)


def transposed_part(local_tiles, row_ids, col_ids, live_slots, panel_rows, col_blocks):
    block_side = local_tiles.shape[1]
    feat_width = panel_rows.shape[-1]
    blocks = panel_rows.reshape(-1, block_side, feat_width)[row_ids]
    products = jnp.einsum("tji,tjf->tif", local_tiles, blocks, preferred_element_type=jnp.float32)
    onehot = jnp.where(
        (col_ids[None, :] == jnp.arange(col_blocks, dtype=jnp.int32)[:, None])
        & live_slots[None, :],
        1.0,
        0.0,
    ).astype(jnp.float32)
    return jnp.einsum("ct,tif->cif", onehot, products).reshape(col_blocks * block_side, feat_width)


def silu_slope(value):
    sigmoid = jax.nn.sigmoid(value)
    return sigmoid * (1.0 + value * (1.0 - sigmoid))


def on_device(features, weight1, weight2, tile_values, tile_coords, tile_count, out_grad):
    local_tiles = tile_values[0, 0]
    row_ids = tile_coords[0, 0, 0]
    col_ids = tile_coords[0, 0, 1]
    slot_total = local_tiles.shape[0]
    live_slots = jnp.arange(slot_total, dtype=jnp.int32) < tile_count[0, 0]
    block_side = local_tiles.shape[1]
    shard_rows = features.shape[1]
    row_blocks = shard_rows * lax.axis_size("col") // block_side
    col_blocks = shard_rows * lax.axis_size("row") // block_side
    node_total = shard_rows * lax.axis_size("row") * lax.axis_size("col")
    grad_local = out_grad[0]
    grad_two = jnp.dot(grad_local, weight2.T, preferred_element_type=jnp.float32).astype(
        jnp.bfloat16
    )
    gathered = lax.all_gather(features, "row", axis=1, tiled=True)[0]
    grad_rows = lax.all_gather(grad_two, "row", axis=0, tiled=True)
    part_one = forward_part(local_tiles, row_ids, col_ids, live_slots, gathered, row_blocks)
    part_three = forward_part(local_tiles, row_ids, col_ids, live_slots, grad_rows, row_blocks)
    agg_sum, grad_hidden = (
        lax.psum_scatter(
            part_one.astype(jnp.bfloat16), "col", scatter_dimension=0, tiled=True
        ).astype(jnp.float32),
        lax.psum_scatter(
            part_three.astype(jnp.bfloat16), "col", scatter_dimension=0, tiled=True
        ).astype(jnp.float32),
    )
    agg_one = agg_sum.astype(jnp.bfloat16)
    pre_one = jnp.dot(agg_one, weight1, preferred_element_type=jnp.float32)
    hidden = jax.nn.silu(pre_one).astype(jnp.bfloat16)
    hidden_rows = lax.all_gather(hidden, "col", axis=0, tiled=True)
    part_two = transposed_part(local_tiles, row_ids, col_ids, live_slots, hidden_rows, col_blocks)
    agg_two = lax.psum_scatter(
        part_two.astype(jnp.bfloat16), "row", scatter_dimension=0, tiled=True
    )
    output = jnp.dot(agg_two, weight2, preferred_element_type=jnp.float32).astype(jnp.bfloat16)
    grad_pre = (grad_hidden * silu_slope(pre_one)).astype(jnp.bfloat16)
    grad_one = jnp.dot(grad_pre, weight1.T, preferred_element_type=jnp.float32).astype(jnp.bfloat16)
    grad_hidden_rows = lax.all_gather(grad_one, "col", axis=0, tiled=True)
    part_four = transposed_part(
        local_tiles, row_ids, col_ids, live_slots, grad_hidden_rows, col_blocks
    )
    grad_features = lax.psum_scatter(
        part_four.astype(jnp.bfloat16), "row", scatter_dimension=0, tiled=True
    )
    contract = (((0,), (0,)), ((), ()))
    weight_one = lax.dot_general(agg_one, grad_pre, contract, preferred_element_type=jnp.float32)
    weight_two = lax.dot_general(agg_two, grad_local, contract, preferred_element_type=jnp.float32)
    sum_one, sum_two = lax.psum((weight_one, weight_two), ("row", "col"))
    factor = 1.0 / math.sqrt(node_total)
    return (output[None], grad_features[None], sum_one * factor, sum_two * factor)


def solution(mesh):
    placed = (
        P("col", "row", None),
        P(),
        P(),
        P("row", "col", None, None, None),
        P("row", "col", None, None),
        P("row", "col"),
        P("col", "row", None),
    )
    return jax.shard_map(
        on_device,
        mesh=mesh,
        in_specs=placed,
        out_specs=(P("col", "row", None), P("col", "row", None), P(), P()),
        check_vma=False,
    )
```

profile of v0, /device:TPU:2, one launch (start us, length us, event | category | flops | bytes accessed | tf_op | source)
XLA Modules:
  0.0 1141.4 jit_solution(11435500891429155768)
XLA Ops:
  7.2 0.0 copy-start
  7.2 0.0 all-gather.5.cloned.1.call-start
  7.2 1.7 convolution_convert_fusion.1
  8.9 0.0 all-gather.5.cloned.1.call-update
  8.9 0.0 all-gather.3.cloned.1.call-start
  9.0 0.7 all-gather.3.cloned.1.call-update
  9.7 0.0 reduce-scatter.9.cloned.1.call-start
  10.4 0.8 fusion.63
  11.2 0.8 slice_bitcast_fusion.1
  11.9 156.6 %all-gather.5.cloned.1.call-done = bf16[4096,128]{1,0:T(8,128)(2,1)} async-done(((bf16[128,128]{1,0:T(8,128)(2,1)}), bf16[4096,128]{1,0:T(8,128)(2,1)}) %all-gather.5.cloned.1.call-update) | async-done | bytes 1048592 | tf_op jit(solution)/shard_map/all_gather | solution.py:57
  168.5 3.9 gather_fusion.2
  172.5 0.0 copy-done
  172.5 5.9 fusion.10
  178.4 5.0 copy.18
  183.3 2.4 fusion.25
  185.8 1.0 copy.14
  186.7 0.0 reduce-scatter.9.cloned.1.call-update
  186.7 0.0 reduce-scatter.5.cloned.1.call-start
  186.8 137.2 %all-gather.3.cloned.1.call-done = bf16[1,4096,128]{2,1,0:T(8,128)(2,1)} async-done(((bf16[1,128,128]{2,1,0:T(8,128)(2,1)}), bf16[1,4096,128]{2,1,0:T(8,128)(2,1)}) %all-gather.3.cloned.1.call-update) | async-done | bytes 1048592 | tf_op jit(solution)/shard_map/all_gather | solution.py:56
  324.0 3.9 gather_fusion
  327.9 5.9 fusion.14
  333.9 5.0 copy.16
  338.8 0.0 copy-start.4
  338.8 2.4 fusion.22
  341.2 1.0 copy.12
  342.2 0.0 reduce-scatter.5.cloned.1.call-update
  342.2 0.0 reduce-scatter.7.cloned.1.call-start
  342.3 71.1 %reduce-scatter.9.cloned.1.call-done = bf16[128,128]{1,0:T(8,128)(2,1)} async-done(((bf16[2048,128]{1,0:T(8,128)(2,1)}), bf16[128,128]{1,0:T(8,128)(2,1)}) %reduce-scatter.9.cloned.1.call-update) | async-done | bytes 32784 | tf_op jit(solution)/shard_map/reduce_scatter | solution.py:64
  413.4 86.4 %reduce-scatter.5.cloned.1.call-done = bf16[128,128]{1,0:T(8,128)(2,1)} async-done(((bf16[2048,128]{1,0:T(8,128)(2,1)}), bf16[128,128]{1,0:T(8,128)(2,1)}) %reduce-scatter.5.cloned.1.call-update) | async-done | bytes 32784 | tf_op jit(solution)/shard_map/reduce_scatter | solution.py:61
  499.8 0.0 copy-done.4
  499.8 0.9 multiply_convert_fusion
  500.8 27.9 %all_gather.13 = bf16[2048,128]{1,0:T(8,128)(2,1)} all-gather(bf16[128,128]{1,0:T(8,128)(2,1)S(1)} %get-tuple-element.7), channel_id=1, replica_groups=mesh['row'=32,'col'=16] {'col'}, dimensions={0}, use_global_device_ids=true | all-gather | bytes 557056 | tf_op jit(solution)/shard_map/all_gather | solution.py:71
  528.7 3.7 gather_fusion.1
  532.4 4.8 fusion.12
  537.2 5.0 copy.17
  542.2 2.4 fusion.16
  544.6 1.4 copy.13
  546.0 0.0 reduce-scatter.7.cloned.1.call-update
  546.0 0.0 all-reduce.3.cloned.1.call-start
  546.1 0.1 convolution_convert_fusion
  546.2 29.6 %all_gather.15 = bf16[2048,128]{1,0:T(8,128)(2,1)} all-gather(bf16[128,128]{1,0:T(8,128)(2,1)S(1)} %convolution_convert_fusion), channel_id=1, replica_groups=mesh['row'=32,'col'=16] {'col'}, dimensions={0}, use_global_device_ids=true | all-gather | bytes 557056 | tf_op jit(solution)/shard_map/all_gather | solution.py:79
  575.8 3.7 gather_fusion.3
  579.6 4.8 fusion.8
  584.4 0.0 copy-start.5
  584.4 0.0 copy-start.2
  584.4 5.0 copy.19
  589.3 0.0 copy-done.5
  589.3 0.8 fusion.72
  590.2 120.2 %reduce-scatter.7.cloned.1.call-done = bf16[128,128]{1,0:T(8,128)(2,1)} async-done(((bf16[4096,128]{1,0:T(8,128)(2,1)}), bf16[128,128]{1,0:T(8,128)(2,1)}) %reduce-scatter.7.cloned.1.call-update) | async-done | bytes 32784 | tf_op jit(solution)/shard_map/reduce_scatter | solution.py:73
  710.4 0.0 copy-done.2
  710.4 1.6 fusion.29
  712.0 0.0 all-reduce.3.cloned.1.call-update
  712.0 0.0 copy-start.1
  712.0 0.0 copy-start.3
  712.0 0.0 reduce-scatter.11.cloned.1.call-start
  712.0 2.4 fusion.19
  714.5 1.4 copy.15
  715.9 0.0 reduce-scatter.11.cloned.1.call-update
  715.9 0.0 copy-done.1
  715.9 0.0 copy-done.3
  715.9 0.8 fusion.28
  716.7 255.6 %all-reduce.3.cloned.1.call-done = (f32[128,128]{1,0:T(8,128)}, f32[128,128]{1,0:T(8,128)}) async-done(((f32[128,128]{1,0:T(8,128)}, f32[128,128]{1,0:T(8,128)}), (f32[128,128]{1,0:T(8,128)}, f32[128,128]{1,0:T(8,128)})) %all-reduce.3.cloned.1.call-update) | async-done | bytes 131088 | tf_op jit(solution)/shard_map/psum | solution.py:89
  972.2 1.5 broadcast_multiply_fusion
  973.8 160.8 %reduce-scatter.11.cloned.1.call-done = bf16[128,128]{1,0:T(8,128)(2,1)} async-done(((bf16[4096,128]{1,0:T(8,128)(2,1)}), bf16[128,128]{1,0:T(8,128)(2,1)}) %reduce-scatter.11.cloned.1.call-update) | async-done | bytes 32784 | tf_op jit(solution)/shard_map/reduce_scatter | solution.py:83
  (3 shorter events, 0.0 us)
Async XLA Ops:
  7.2 165.3 %copy-start = (bf16[1,1,96,128,128]{4,3,2,1,0:T(8,128)(2,1)S(1)}, bf16[1,1,96,128,128]{4,3,2,1,0:T(8,128)(2,1)}, u32[]{:S(2)}) copy-start(bf16[1,1,96,128,128]{4,3,2,1,0:T(8,128)(2,1)} %param.10) | copy-start | bytes 9437188
  7.2 161.4 %all-gather.5.cloned.1.call-start = ((), (), s32[]{:S(2)}) async-start(), calls=%async_computation.7 | async-start | bytes 1081344 | tf_op jit(solution)/shard_map/all_gather | solution.py:57
  8.9 315.1 %all-gather.3.cloned.1.call-start = ((), (), s32[]{:S(2)}) async-start(), calls=%async_computation.4 | async-start | bytes 1081344 | tf_op jit(solution)/shard_map/all_gather | solution.py:56
  9.7 403.7 %reduce-scatter.9.cloned.1.call-start = ((), (), s32[]{:S(2)}) async-start(), calls=%async_computation.8 | async-start | bytes 557056 | tf_op jit(solution)/shard_map/reduce_scatter | solution.py:64
  186.7 313.1 %reduce-scatter.5.cloned.1.call-start = ((), (), s32[]{:S(2)}) async-start(), calls=%async_computation.5 | async-start | bytes 557056 | tf_op jit(solution)/shard_map/reduce_scatter | solution.py:61
  338.8 161.0 %copy-start.4 = (bf16[128,128]{1,0:T(8,128)(2,1)S(1)}, bf16[128,128]{1,0:T(8,128)(2,1)}, u32[]{:S(2)}) copy-start(bf16[128,128]{1,0:T(8,128)(2,1)} %param.8) | copy-start | bytes 98308
  342.2 368.2 %reduce-scatter.7.cloned.1.call-start = ((), (), s32[]{:S(2)}) async-start(), calls=%async_computation.6 | async-start | bytes 1081344 | tf_op jit(solution)/shard_map/reduce_scatter | solution.py:73
  546.0 426.2 %all-reduce.3.cloned.1.call-start = ((), (), s32[]{:S(2)}) async-start(), calls=%async_computation.10 | async-start | bytes 262144 | tf_op jit(solution)/shard_map/psum | solution.py:89
  584.4 5.0 copy-start.5
  584.4 126.0 %copy-start.2 = (bf16[1,128,128]{2,1,0:T(8,128)(2,1)S(1)}, bf16[1,128,128]{2,1,0:T(8,128)(2,1)}, u32[]{:S(2)}) copy-start(bf16[1,128,128]{2,1,0:T(8,128)(2,1)} %param.13) | copy-start | bytes 98308
  712.0 3.9 copy-start.1
  712.0 3.9 copy-start.3
  712.0 422.6 %reduce-scatter.11.cloned.1.call-start = ((), (), s32[]{:S(2)}) async-start(), calls=%async_computation.9 | async-start | bytes 1081344 | tf_op jit(solution)/shard_map/reduce_scatter | solution.py:83
Sparse Core Ops, SparseCore 0:
  10.7 157.8 all-gather.4
  170.6 153.3 all-gather.2
  328.7 84.6 reduce-scatter.8
  418.5 81.2 reduce-scatter.4
  546.1 164.1 reduce-scatter.6
  716.9 255.3 all-reduce.2
  975.6 158.9 reduce-scatter.10
where the time goes:
time: 1140 us
  waiting for transfers between devices  989 us (87%)
  blocking collectives  57.6 us (5%)
  local copies, waits for them, and re-layouts  40.6 us (4%)
  matrix products  37 us (3%)
  between operations  14.9 us (1%)
    psum x1, waiting for transfers between devices, on_device(): sum_one, sum_two = lax.psum((weight_one, weight_two), ('row', 'col'))  256 us
    reduce_scatter x1, waiting for transfers between devices, on_device(): lax.psum_scatter(part_four.astype(jnp.bfloat16), 'row', scatter_dimension...  161 us
    all_gather x1, waiting for transfers between devices, on_device(): grad_rows = lax.all_gather(grad_two, 'row', axis=0, tiled=True)  157 us
    all_gather x1, waiting for transfers between devices, on_device(): gathered = lax.all_gather(features, 'row', axis=1, tiled=True)[0]  137 us
    reduce_scatter x1, waiting for transfers between devices, on_device(): lax.psum_scatter(part_two.astype(jnp.bfloat16), 'row', scatter_dimension=...  120 us
    reduce_scatter x1, waiting for transfers between devices, on_device(): lax.psum_scatter(part_one.astype(jnp.bfloat16), 'col', scatter_dimension=...  86.4 us
    reduce_scatter x1, waiting for transfers between devices, on_device(): lax.psum_scatter(part_three.astype(jnp.bfloat16), 'col', scatter_dimensio...  71.1 us
    all_gather x1, blocking collectives, on_device(): grad_hidden_rows = lax.all_gather(grad_one, 'col', axis=0, tiled=True)  29.6 us
  transfers between devices with their start and end apart: 7, of which 7 were waited for; matrix products, arithmetic and copies ran while one was open for 5% of the time, Pallas kernels for 0%

commit v1 on v0

--- a/solution.py
+++ b/solution.py
@@ -86,7 +86,7 @@
     contract = (((0,), (0,)), ((), ()))
     weight_one = lax.dot_general(agg_one, grad_pre, contract, preferred_element_type=jnp.float32)
     weight_two = lax.dot_general(agg_two, grad_local, contract, preferred_element_type=jnp.float32)
-    sum_one, sum_two = lax.psum((weight_one, weight_two), ("row", "col"))
+    sum_one, sum_two = lax.psum(lax.psum((weight_one, weight_two), "col"), "row")
     factor = 1.0 / math.sqrt(node_total)
     return (output[None], grad_features[None], sum_one * factor, sum_two * factor)
 

time: 1140 us -> 1350 us (1.18)
  the two profiles are of different devices: /device:TPU:2 before, /device:TPU:4 now
where the time goes in v1:
time: 1350 us
  waiting for transfers between devices  1200 us (89%)
  blocking collectives  55.4 us (4%)
  local copies, waits for them, and re-layouts  40.5 us (3%)
  matrix products  37 us (3%)
  between operations  14.9 us (1%)
    psum x1, waiting for transfers between devices, on_device(): lax.psum(lax.psum((weight_one, weight_two), 'col'), 'row')  291 us
    reduce_scatter x1, waiting for transfers between devices, on_device(): lax.psum_scatter(part_four.astype(jnp.bfloat16), 'row', scatter_dimension...  163 us
    psum x1, waiting for transfers between devices, on_device(): lax.psum((weight_one, weight_two), 'col')  159 us
    all_gather x1, waiting for transfers between devices, on_device(): grad_rows = lax.all_gather(grad_two, 'row', axis=0, tiled=True)  157 us
    all_gather x1, waiting for transfers between devices, on_device(): gathered = lax.all_gather(features, 'row', axis=1, tiled=True)[0]  137 us
    reduce_scatter x1, waiting for transfers between devices, on_device(): lax.psum_scatter(part_two.astype(jnp.bfloat16), 'row', scatter_dimension=...  133 us
    reduce_scatter x1, waiting for transfers between devices, on_device(): lax.psum_scatter(part_one.astype(jnp.bfloat16), 'col', scatter_dimension=...  86.5 us
    reduce_scatter x1, waiting for transfers between devices, on_device(): lax.psum_scatter(part_three.astype(jnp.bfloat16), 'col', scatter_dimensio...  69.6 us
  transfers between devices with their start and end apart: 8, of which 8 were waited for; matrix products, arithmetic and copies ran while one was open for 4% of the time, Pallas kernels for 0%

profile of v1, /device:TPU:4, one launch (start us, length us, event | category | flops | bytes accessed | tf_op | source)
XLA Modules:
  0.0 1347.5 jit_solution(6429198725798403510)
XLA Ops:
  7.2 0.0 copy-start
  7.2 0.0 all-gather.5.cloned.1.call-start
  7.2 1.7 convolution_convert_fusion.1
  8.9 0.0 all-gather.5.cloned.1.call-update
  8.9 0.0 all-gather.3.cloned.1.call-start
  9.0 0.7 all-gather.3.cloned.1.call-update
  9.7 0.0 reduce-scatter.9.cloned.1.call-start
  10.4 0.8 fusion.63
  11.2 0.8 slice_bitcast_fusion.1
  11.9 156.7 %all-gather.5.cloned.1.call-done = bf16[4096,128]{1,0:T(8,128)(2,1)} async-done(((bf16[128,128]{1,0:T(8,128)(2,1)}), bf16[4096,128]{1,0:T(8,128)(2,1)}) %all-gather.5.cloned.1.call-update) | async-done | bytes 1048592 | tf_op jit(solution)/shard_map/all_gather | solution.py:57
  168.6 3.9 gather_fusion.2
  172.6 0.0 copy-done
  172.6 5.9 fusion.10
  178.5 4.9 copy.18
  183.4 2.4 fusion.25
  185.8 1.0 copy.14
  186.8 0.0 reduce-scatter.9.cloned.1.call-update
  186.8 0.0 reduce-scatter.5.cloned.1.call-start
  186.9 137.4 %all-gather.3.cloned.1.call-done = bf16[1,4096,128]{2,1,0:T(8,128)(2,1)} async-done(((bf16[1,128,128]{2,1,0:T(8,128)(2,1)}), bf16[1,4096,128]{2,1,0:T(8,128)(2,1)}) %all-gather.3.cloned.1.call-update) | async-done | bytes 1048592 | tf_op jit(solution)/shard_map/all_gather | solution.py:56
  324.3 3.9 gather_fusion
  328.2 5.9 fusion.14
  334.1 4.9 copy.16
  339.0 2.4 fusion.22
  341.4 0.9 copy.12
  342.4 0.0 reduce-scatter.5.cloned.1.call-update
  342.4 0.0 reduce-scatter.7.cloned.1.call-start
  342.5 69.6 %reduce-scatter.9.cloned.1.call-done = bf16[128,128]{1,0:T(8,128)(2,1)} async-done(((bf16[2048,128]{1,0:T(8,128)(2,1)}), bf16[128,128]{1,0:T(8,128)(2,1)}) %reduce-scatter.9.cloned.1.call-update) | async-done | bytes 32784 | tf_op jit(solution)/shard_map/reduce_scatter | solution.py:64
  412.1 86.5 %reduce-scatter.5.cloned.1.call-done = bf16[128,128]{1,0:T(8,128)(2,1)} async-done(((bf16[2048,128]{1,0:T(8,128)(2,1)}), bf16[128,128]{1,0:T(8,128)(2,1)}) %reduce-scatter.5.cloned.1.call-update) | async-done | bytes 32784 | tf_op jit(solution)/shard_map/reduce_scatter | solution.py:61
  498.6 0.0 copy-done.4
  498.6 0.9 multiply_convert_fusion
  499.5 24.0 %all_gather.13 = bf16[2048,128]{1,0:T(8,128)(2,1)} all-gather(bf16[128,128]{1,0:T(8,128)(2,1)S(1)} %get-tuple-element.9), channel_id=1, replica_groups=mesh['row'=32,'col'=16] {'col'}, dimensions={0}, use_global_device_ids=true | all-gather | bytes 557056 | tf_op jit(solution)/shard_map/all_gather | solution.py:71
  523.6 3.7 gather_fusion.1
  527.3 4.8 fusion.12
  532.1 4.9 copy.17
  537.0 2.4 fusion.16
  539.4 1.4 copy.13
  540.9 0.0 reduce-scatter.7.cloned.1.call-update
  540.9 0.0 all-reduce.7.cloned.1.call-start
  540.9 0.1 convolution_convert_fusion
  541.1 31.4 %all_gather.15 = bf16[2048,128]{1,0:T(8,128)(2,1)} all-gather(bf16[128,128]{1,0:T(8,128)(2,1)S(1)} %convolution_convert_fusion), channel_id=1, replica_groups=mesh['row'=32,'col'=16] {'col'}, dimensions={0}, use_global_device_ids=true | all-gather | bytes 557056 | tf_op jit(solution)/shard_map/all_gather | solution.py:79
  572.5 3.8 gather_fusion.3
  576.2 0.0 copy-done.5
  576.2 0.8 fusion.72
  577.0 132.8 %reduce-scatter.7.cloned.1.call-done = bf16[128,128]{1,0:T(8,128)(2,1)} async-done(((bf16[4096,128]{1,0:T(8,128)(2,1)}), bf16[128,128]{1,0:T(8,128)(2,1)}) %reduce-scatter.7.cloned.1.call-update) | async-done | bytes 32784 | tf_op jit(solution)/shard_map/reduce_scatter | solution.py:73
  709.8 0.0 copy-done.2
  709.8 1.6 fusion.29
  711.4 0.0 all-reduce.7.cloned.1.call-update
  711.4 0.2 all-reduce.5.cloned.1.call-start
  711.7 4.8 fusion.8
  716.4 4.9 copy.19
  721.4 159.5 %all-reduce.7.cloned.1.call-done = (f32[128,128]{1,0:T(8,128)}, f32[128,128]{1,0:T(8,128)}) async-done(((f32[128,128]{1,0:T(8,128)}, f32[128,128]{1,0:T(8,128)}), (f32[128,128]{1,0:T(8,128)}, f32[128,128]{1,0:T(8,128)})) %all-reduce.7.cloned.1.call-update) | async-done | bytes 131088 | tf_op jit(solution)/shard_map/psum | solution.py:89
  880.8 0.0 all-reduce.5.cloned.1.call-update
  880.9 0.0 copy-start.1
  880.9 0.0 copy-start.3
  880.9 0.0 reduce-scatter.11.cloned.1.call-start
  880.9 2.4 fusion.19
  883.4 1.4 copy.15
  884.8 0.0 reduce-scatter.11.cloned.1.call-update
  884.8 0.0 copy-done.1
  884.8 0.0 copy-done.3
  884.8 0.8 fusion.28
  885.6 290.9 %all-reduce.5.cloned.1.call-done = (f32[128,128]{1,0:T(8,128)}, f32[128,128]{1,0:T(8,128)}) async-done(((f32[128,128]{1,0:T(8,128)}, f32[128,128]{1,0:T(8,128)}), (f32[128,128]{1,0:T(8,128)}, f32[128,128]{1,0:T(8,128)})) %all-reduce.5.cloned.1.call-update) | async-done | bytes 131088 | tf_op jit(solution)/shard_map/psum | solution.py:89
  1176.5 1.5 broadcast_multiply_fusion
  1178.0 162.7 %reduce-scatter.11.cloned.1.call-done = bf16[128,128]{1,0:T(8,128)(2,1)} async-done(((bf16[4096,128]{1,0:T(8,128)(2,1)}), bf16[128,128]{1,0:T(8,128)(2,1)}) %reduce-scatter.11.cloned.1.call-update) | async-done | bytes 32784 | tf_op jit(solution)/shard_map/reduce_scatter | solution.py:83
  (6 shorter events, 0.0 us)
Async XLA Ops:
  7.2 165.4 %copy-start = (bf16[1,1,96,128,128]{4,3,2,1,0:T(8,128)(2,1)S(1)}, bf16[1,1,96,128,128]{4,3,2,1,0:T(8,128)(2,1)}, u32[]{:S(2)}) copy-start(bf16[1,1,96,128,128]{4,3,2,1,0:T(8,128)(2,1)} %param.10) | copy-start | bytes 9437188
  7.2 161.4 %all-gather.5.cloned.1.call-start = ((), (), s32[]{:S(2)}) async-start(), calls=%async_computation.7 | async-start | bytes 1081344 | tf_op jit(solution)/shard_map/all_gather | solution.py:57
  8.9 315.3 %all-gather.3.cloned.1.call-start = ((), (), s32[]{:S(2)}) async-start(), calls=%async_computation.4 | async-start | bytes 1081344 | tf_op jit(solution)/shard_map/all_gather | solution.py:56
  9.7 402.4 %reduce-scatter.9.cloned.1.call-start = ((), (), s32[]{:S(2)}) async-start(), calls=%async_computation.8 | async-start | bytes 557056 | tf_op jit(solution)/shard_map/reduce_scatter | solution.py:64
  186.8 311.8 %reduce-scatter.5.cloned.1.call-start = ((), (), s32[]{:S(2)}) async-start(), calls=%async_computation.5 | async-start | bytes 557056 | tf_op jit(solution)/shard_map/reduce_scatter | solution.py:61
  339.0 159.5 %copy-start.4 = (bf16[128,128]{1,0:T(8,128)(2,1)S(1)}, bf16[128,128]{1,0:T(8,128)(2,1)}, u32[]{:S(2)}) copy-start(bf16[128,128]{1,0:T(8,128)(2,1)} %param.8) | copy-start | bytes 98308
  342.4 367.4 %reduce-scatter.7.cloned.1.call-start = ((), (), s32[]{:S(2)}) async-start(), calls=%async_computation.6 | async-start | bytes 1081344 | tf_op jit(solution)/shard_map/reduce_scatter | solution.py:73
  540.9 340.0 %all-reduce.7.cloned.1.call-start = ((), (), s32[]{:S(2)}) async-start(), calls=%async_computation.11 | async-start | bytes 262144 | tf_op jit(solution)/shard_map/psum | solution.py:89
  572.5 3.8 copy-start.5
  572.5 137.4 %copy-start.2 = (bf16[1,128,128]{2,1,0:T(8,128)(2,1)S(1)}, bf16[1,128,128]{2,1,0:T(8,128)(2,1)}, u32[]{:S(2)}) copy-start(bf16[1,128,128]{2,1,0:T(8,128)(2,1)} %param.13) | copy-start | bytes 98308
  711.4 465.1 %all-reduce.5.cloned.1.call-start = ((), (), s32[]{:S(2)}) async-start(), calls=%async_computation.10 | async-start | bytes 262144 | tf_op jit(solution)/shard_map/psum | solution.py:89
  880.9 3.9 copy-start.1
  880.9 3.9 copy-start.3
  880.9 459.8 %reduce-scatter.11.cloned.1.call-start = ((), (), s32[]{:S(2)}) async-start(), calls=%async_computation.9 | async-start | bytes 1081344 | tf_op jit(solution)/shard_map/reduce_scatter | solution.py:83
Sparse Core Ops, SparseCore 0:
  10.7 157.9 all-gather.4
  170.7 153.4 all-gather.2
  328.9 83.1 reduce-scatter.8
  417.2 81.2 reduce-scatter.4
  541.0 168.7 reduce-scatter.6
  713.5 167.3 all-reduce.6
  883.8 292.6 all-reduce.4
  1180.1 160.5 reduce-scatter.10
